TPU v7x, 32 devices: a whole 2x2x4 slice. The times are simulated.
32 devices in a mesh: dp: 2 (over y), tm: 8 (over z, x), height: 2 (over core).
Axes of the slice: x: 2, y: 2, z: 4, core: 2. Of those that a mesh axis runs over, the one named last changes fastest.
Arguments:
- queries: bfloat16 [2, 16, 16, 8, 1536], P('dp', 'tm', 'height'), may hold values from -6 to 6
- keys: bfloat16 [2, 16, 16, 8, 1536], P('dp', 'tm', 'height'), may hold values from -6 to 6
- values: bfloat16 [2, 16, 16, 8, 1536], P('dp', 'tm', 'height'), may hold values from -6 to 6
- text_keys: bfloat16 [2, 256, 1536], P('dp'), may hold values from -110 to 110
- text_values: bfloat16 [2, 256, 1536], P('dp'), may hold values from -6 to 6
- gain_q: float32 [128], replicated, may hold values from 0.5 to 1.5
- gain_k: float32 [128], replicated, may hold values from 0.5 to 1.5
- window_ext: int32 [12, 3], replicated, may hold values from 0 to 1, as said below
- text_len: int32 [2], P('dp'), may hold values from 64 to 256, as said below
- out_grad: bfloat16 [2, 16, 16, 8, 1536], P('dp', 'tm', 'height'), may hold values from -60 to 60
Outputs:
- query_grad: bfloat16 [2, 16, 16, 8, 1536], P('dp', 'tm', 'height')
- key_grad: bfloat16 [2, 16, 16, 8, 1536], P('dp', 'tm', 'height')
- value_grad: bfloat16 [2, 16, 16, 8, 1536], P('dp', 'tm', 'height')
- text_key_grad: float32 [2, 256, 1536], P('dp')
- text_value_grad: float32 [2, 256, 1536], P('dp')
- gain_grads: float32 [2, 128], replicated
Inputs may be any that keep to these rules, and one draw needn't show every extreme that they name: `window_ext`: along each of the three axes some head has reach 1. `text_len`: some sample has all 256 text tokens live.
All inputs are finite; a program needn't handle non-finite values.
Results may differ from a plain program's by a relative error of at most 0.0055.
The roundings to bfloat16 on the way count: a program that leaves them out, or rounds other values in their place, can miss the bound.
Values may be sent and summed in bfloat16 or wider, within the bound.
No kernel may reach another device: no remote copies, remote signals or barrier semaphores. Data moves between devices by JAX's collectives and lax.ppermute only.
A program may use at most 128 MiB of HBM per device.

v0:
```python
import jax
import jax.numpy as jnp
from jax import lax
from jax.sharding import PartitionSpec as P

TILE_F = 2
TILE_H = 4
TILE_W = 4
EPS = 1e-06


def extended(x, sides, width):
    for axis, dim in sides:
        peers, length = (lax.axis_size(axis), x.shape[dim])
        up = [(i, (i + 1) % peers) for i in range(peers - 1)]
        down = [(j, i) for i, j in up]
        last = lax.slice_in_dim(x, length - width, length, axis=dim)
        first = lax.slice_in_dim(x, 0, width, axis=dim)
        before = lax.ppermute(last, axis, up)
        after = lax.ppermute(first, axis, down)
        x = jnp.concatenate([before, x, after], axis=dim)
    return x


def normalize(raw_values, gain_vector, head_count):
    full_shape = raw_values.shape
    head_size = gain_vector.shape[0]
    split_values = raw_values.astype(jnp.float32).reshape(full_shape[:-1] + (head_count, head_size))
    inverse = lax.rsqrt(jnp.mean(split_values * split_values, axis=-1, keepdims=True) + EPS)
    scaled = (split_values * inverse * gain_vector).reshape(full_shape).astype(jnp.bfloat16)
    return (scaled, split_values, inverse)


def norm_backward(grad_out, split_values, inverse, gain_vector):
    full_shape = grad_out.shape
    grad_split = grad_out.reshape(split_values.shape)
    weighted = grad_split * gain_vector
    inner_mean = jnp.mean(weighted * split_values, axis=-1, keepdims=True)
    grad_in = inverse * weighted - split_values * (inverse * inverse * inverse) * inner_mean
    gain_term = jnp.sum(
        (grad_split * split_values * inverse).reshape(-1, gain_vector.shape[0]), axis=0
    )
    return (grad_in.reshape(full_shape), gain_term)


def head_grads(query_head, key_head, value_head, grad_head, allowed):
    score_scale = query_head.shape[-1] ** (-0.5)
    scores = jnp.dot(query_head, key_head.T, preferred_element_type=jnp.float32) * score_scale
    scores = jnp.where(allowed, scores, -1e30)
    peak_score = jnp.max(scores, axis=-1, keepdims=True)
    weights = jnp.exp(scores - peak_score)
    weights = weights / jnp.sum(weights, axis=-1, keepdims=True)
    weights_low = weights.astype(jnp.bfloat16)
    output = jnp.dot(weights_low, value_head, preferred_element_type=jnp.float32)
    delta_row = jnp.sum(grad_head.astype(jnp.float32) * output, axis=-1, keepdims=True)
    value_part = jnp.dot(weights_low.T, grad_head, preferred_element_type=jnp.float32)
    prob_grad = jnp.dot(grad_head, value_head.T, preferred_element_type=jnp.float32)
    score_grad = (weights * (prob_grad - delta_row)).astype(jnp.bfloat16)
    query_part = jnp.dot(score_grad, key_head, preferred_element_type=jnp.float32) * score_scale
    key_part = jnp.dot(score_grad.T, query_head, preferred_element_type=jnp.float32) * score_scale
    return (query_part, key_part, value_part)


def split_heads(matrix, head_count):
    return matrix.reshape(matrix.shape[0], head_count, -1).transpose(1, 0, 2)


def merge_heads(stacked):
    return stacked.transpose(1, 0, 2).reshape(stacked.shape[1], -1)


def tile_window(first_tiles, second_tiles, extent):
    within = jnp.abs(first_tiles[:, None, 0] - second_tiles[None, :, 0]) <= extent[0]
    within = within & (jnp.abs(first_tiles[:, None, 1] - second_tiles[None, :, 1]) <= extent[1])
    return within & (jnp.abs(first_tiles[:, None, 2] - second_tiles[None, :, 2]) <= extent[2])


def allowed_mask(query_tiles, key_tiles, key_valid, text_valid, extent):
    within = tile_window(query_tiles, key_tiles, extent)
    video_mask = within & key_valid[None, :]
    text_mask = jnp.broadcast_to(text_valid[None, :], (query_tiles.shape[0], text_valid.shape[0]))
    return jnp.concatenate([video_mask, text_mask], axis=1)


def attend_all(
    query_flat,
    key_flat,
    value_flat,
    grad_flat,
    extents,
    query_tiles,
    key_tiles,
    key_valid,
    text_valid,
):
    head_count = extents.shape[0]

    def per_head(operands):
        query_head, key_head, value_head, grad_head, extent = operands
        allowed = allowed_mask(query_tiles, key_tiles, key_valid, text_valid, extent)
        return head_grads(query_head, key_head, value_head, grad_head, allowed)

    grad_query, grad_keys, grad_values = lax.map(
        per_head,
        (
            split_heads(query_flat, head_count),
            split_heads(key_flat, head_count),
            split_heads(value_flat, head_count),
            split_heads(grad_flat, head_count),
            extents,
        ),
    )
    return (merge_heads(grad_query), merge_heads(grad_keys), merge_heads(grad_values))


def tile_coords(frame_index, row_index, column_index):
    full_shape = (frame_index.shape[0], row_index.shape[0], column_index.shape[0])
    pieces = [
        jnp.broadcast_to((frame_index // TILE_F)[:, None, None], full_shape),
        jnp.broadcast_to((row_index // TILE_H)[None, :, None], full_shape),
        jnp.broadcast_to((column_index // TILE_W)[None, None, :], full_shape),
    ]
    return jnp.stack(pieces, axis=-1).reshape(-1, 3)


def fold_axis(array, axis_number, width, inner_count):
    owned = lax.slice_in_dim(array, 2 * width, 2 * width + inner_count, axis=axis_number)
    lower = lax.slice_in_dim(array, 0, width, axis=axis_number)
    upper = lax.slice_in_dim(
        array, inner_count + 3 * width, inner_count + 4 * width, axis=axis_number
    )
    low_pad = [(0, 0)] * array.ndim
    high_pad = [(0, 0)] * array.ndim
    low_pad[axis_number] = (0, inner_count - width)
    high_pad[axis_number] = (inner_count - width, 0)
    return owned + jnp.pad(lower, low_pad) + jnp.pad(upper, high_pad)


def local(
    queries, keys, values, text_keys, text_values, gain_q, gain_k, window_ext, text_len, out_grad
):
    head_count = window_ext.shape[0]
    frame_count, row_count, column_count, feature_count = queries.shape[1:]
    text_count = text_keys.shape[1]
    frame_base = lax.axis_index("tm") * frame_count
    row_base = lax.axis_index("height") * row_count
    total_frames = frame_count * lax.axis_size("tm")
    total_rows = row_count * lax.axis_size("height")
    query_norm, query_split, query_inverse = normalize(queries[0], gain_q, head_count)
    key_norm, key_split, key_inverse = normalize(keys[0], gain_k, head_count)
    stacked = jnp.stack([key_norm, values[0]])
    rowed = extended(stacked, (("height", 2),), TILE_H)
    beside_all = extended(rowed, (("tm", 1),), TILE_F)
    frames_wide = frame_count + 2 * TILE_F
    rows_wide = row_count + 2 * TILE_H
    column_index = jnp.arange(column_count)
    query_frames = frame_base + jnp.arange(frame_count)
    query_rows = row_base + jnp.arange(row_count)
    key_frames = frame_base - TILE_F + jnp.arange(frames_wide)
    key_rows = row_base - TILE_H + jnp.arange(rows_wide)
    query_tiles = tile_coords(query_frames, query_rows, column_index)
    key_tiles = tile_coords(key_frames, key_rows, column_index)
    frame_valid = (key_frames >= 0) & (key_frames < total_frames)
    row_valid = (key_rows >= 0) & (key_rows < total_rows)
    key_valid = jnp.broadcast_to(
        frame_valid[:, None, None] & row_valid[None, :, None],
        (frames_wide, rows_wide, column_count),
    ).reshape(-1)
    text_valid = jnp.arange(text_count) < text_len[0]
    key_all = jnp.concatenate([beside_all[0].reshape(-1, feature_count), text_keys[0]], axis=0)
    value_all = jnp.concatenate([beside_all[1].reshape(-1, feature_count), text_values[0]], axis=0)
    query_flat = query_norm.reshape(-1, feature_count)
    grad_flat = out_grad[0].reshape(-1, feature_count)
    video_count = frames_wide * rows_wide * column_count
    grad_query, grad_keys, grad_values = attend_all(
        query_flat,
        key_all,
        value_all,
        grad_flat,
        window_ext,
        query_tiles,
        key_tiles,
        key_valid,
        text_valid,
    )
    grads = jnp.stack([grad_keys[:video_count], grad_values[:video_count]]).reshape(
        2, frames_wide, rows_wide, column_count, feature_count
    )
    returned = extended(grads, (("tm", 1),), TILE_F)
    partial_sum = fold_axis(returned, 1, TILE_F, frame_count)
    returned_rows = extended(partial_sum, (("height", 2),), TILE_H)
    owned = fold_axis(returned_rows, 2, TILE_H, row_count)
    key_own = owned[0]
    value_own = owned[1]
    text_key_part = grad_keys[video_count:]
    text_value_part = grad_values[video_count:]
    query_full = grad_query.reshape(frame_count, row_count, column_count, feature_count)
    query_out, query_gain = norm_backward(query_full, query_split, query_inverse, gain_q)
    key_out, key_gain = norm_backward(key_own, key_split, key_inverse, gain_k)
    gain_terms = jnp.stack([query_gain, key_gain])
    text_key_sum, text_value_sum = lax.psum((text_key_part, text_value_part), ("tm", "height"))
    gain_total = lax.psum(gain_terms, ("dp", "tm", "height"))
    return (
        query_out.astype(jnp.bfloat16)[None],
        key_out.astype(jnp.bfloat16)[None],
        value_own.astype(jnp.bfloat16)[None],
        text_key_sum[None],
        text_value_sum[None],
        gain_total,
    )


def solution(mesh):
    return jax.shard_map(
        local,
        mesh=mesh,
        in_specs=(
            P("dp", "tm", "height", None, None),
            P("dp", "tm", "height", None, None),
            P("dp", "tm", "height", None, None),
            P("dp", None, None),
            P("dp", None, None),
            P(),
            P(),
            P(),
            P("dp"),
            P("dp", "tm", "height", None, None),
        ),
        out_specs=(
            P("dp", "tm", "height", None, None),
            P("dp", "tm", "height", None, None),
            P("dp", "tm", "height", None, None),
            P("dp", None, None),
            P("dp", None, None),
            P(),
        ),
        check_vma=False,
    )
```

profile of v0, /device:TPU:0, one launch (start us, length us, event | category | flops | bytes accessed | tf_op | source)
XLA Modules:
  0.0 574.4 jit_solution(11806287769408357860)
XLA Ops:
  12.3 2.4 collective-permute-start
  16.1 2.3 collective-permute-done.1
  21.0 6.0 %collective-permute-start.2 = (bf16[2,2,16,8,1536]{4,3,2,1,0:T(8,128)(2,1)}, bf16[2,2,16,8,1536]{4,3,2,1,0:T(8,128)(2,1)}, u32[]{:S(2)}, u32[]{:S(2)}) collective-permute-start(bf16[2,2,16,8,1536]{4,3,2,1,0:T(8,128)(2,1)} %pad_maximum_fusion.1), channel_id=1, source_target_pairs={{0,2},{2,4},{4,6},{6,8},{8,10},{10,12},{12,14},{1,3},{3,5},{5,7},{... | collective-permute-start | bytes 4718600 | tf_op jit(solution)/shard_map/ppermute | solution.py:19
  33.6 1.9 copy.74
  37.0 1.7 copy.76
  40.6 18.4 %collective-permute-done.3 = bf16[2,2,16,8,1536]{4,3,2,1,0:T(8,128)(2,1)} collective-permute-done((bf16[2,2,16,8,1536]{4,3,2,1,0:T(8,128)(2,1)}, bf16[2,2,16,8,1536]{4,3,2,1,0:T(8,128)(2,1)}, u32[]{:S(2)}, u32[]{:S(2)}) %collective-permute-start.3) | collective-permute-done | bytes 1572896 | tf_op jit(solution)/shard_map/ppermute | solution.py:20
  59.0 33.9 %collective-permute-done.2 = bf16[2,2,16,8,1536]{4,3,2,1,0:T(8,128)(2,1)} collective-permute-done((bf16[2,2,16,8,1536]{4,3,2,1,0:T(8,128)(2,1)}, bf16[2,2,16,8,1536]{4,3,2,1,0:T(8,128)(2,1)}, u32[]{:S(2)}, u32[]{:S(2)}) %collective-permute-start.2) | collective-permute-done | bytes 1572896 | tf_op jit(solution)/shard_map/ppermute | solution.py:19
  92.8 3.0 pad_maximum_fusion
  95.8 2.8 fusion.59
  98.6 4.2 concatenate.31
  102.7 1.9 maximum_bitcast_fusion.1
  104.6 2.4 copy.80
  107.1 4.2 concatenate.28
  111.2 1.9 maximum_bitcast_fusion
  113.2 2.5 copy.78
  115.7 173.7 %while.15 = (s32[]{:T(128)}, f32[12,128,128]{2,0,1:T(8,128)S(1)}, f32[12,1024,128]{1,2,0:T(8,128)}, f32[12,1024,128]{1,2,0:T(8,128)}, s32[128,3]{0,1:T(4,128)S(1...) while((s32[]{:T(128)}, f32[12,128,128]{2,0,1:T(8,128)S(1)}, ...), condition=%wide.region_6.7_spmd.clone, body=%wide.region_2.6_spmd.clone.sunk | while | flops 204930944 | bytes 8207186 | solution.py:103
  117.2 2.3 fusion.92
  127.4 1.9 fusion.98
  131.7 2.3 fusion.92
  141.9 1.9 fusion.98
  146.2 2.3 fusion.92
  156.4 1.9 fusion.98
  160.6 2.3 fusion.92
  170.9 1.9 fusion.98
  175.1 2.3 fusion.92
  185.3 1.9 fusion.98
  189.6 2.3 fusion.92
  199.8 1.9 fusion.98
  204.0 2.3 fusion.92
  214.3 1.9 fusion.98
  218.5 2.3 fusion.92
  228.7 1.9 fusion.98
  233.0 2.3 fusion.92
  243.2 1.9 fusion.98
  247.5 2.3 fusion.92
  257.7 1.9 fusion.98
  261.9 2.3 fusion.92
  272.2 1.9 fusion.98
  276.4 2.3 fusion.92
  286.6 1.9 fusion.98
  289.4 5.2 slice.118
  294.5 6.6 %copy.85 = f32[768,12,128]{2,1,0:T(8,128)} copy(f32[768,12,128]{0,2,1:T(8,128)} %slice.118) | data formatting | bytes 9437184 | tf_op jit(solution)/shard_map/slice | solution.py:186
  301.2 6.8 %stack.31 = f32[1,6,16,8,1536]{4,3,2,1,0:T(8,128)} reshape(f32[768,12,128]{2,1,0:T(8,128)} %copy.85) | data formatting | bytes 9437184 | tf_op jit(solution)/shard_map/stack | solution.py:186
  307.9 4.9 slice.119
  312.8 6.6 %copy.87 = f32[768,12,128]{2,1,0:T(8,128)} copy(f32[768,12,128]{0,2,1:T(8,128)} %slice.119) | data formatting | bytes 9437184 | tf_op jit(solution)/shard_map/slice | solution.py:186
  319.4 6.8 %stack.32 = f32[1,6,16,8,1536]{4,3,2,1,0:T(8,128)} reshape(f32[768,12,128]{2,1,0:T(8,128)} %copy.87) | data formatting | bytes 9437184 | tf_op jit(solution)/shard_map/stack | solution.py:186
  326.1 2.8 constant_dynamic-update-slice_fusion.2
  330.2 3.4 fusion.58
  333.6 2.2 copy-done
  335.8 4.8 collective-permute-start.4
  342.0 1.7 copy.88
  345.2 2.7 slice.128
  347.9 2.7 slice.129
  350.6 141.3 %collective-permute-done.4 = f32[2,2,16,8,1536]{4,3,2,1,0:T(8,128)S(1)} collective-permute-done((f32[2,2,16,8,1536]{4,3,2,1,0:T(8,128)}, f32[2,2,16,8,1536]{4,3,2,1,0:T(8,128)S(1)}, u32[]{:S(2)}, u32[]{:S(2)}) %collective-permute-start.4) | collective-permute-done | bytes 3145760 | tf_op jit(solution)/shard_map/ppermute | solution.py:19
  491.9 1.7 copy-done.10
  493.5 4.8 fusion.41
  499.7 2.2 collective-permute-start.6
  508.7 1.6 copy.83
  510.3 2.2 reshape_reshape_reshape.3
  512.6 2.6 fusion.53
  515.2 3.0 copy.89
  518.3 3.0 copy.90
  521.3 1.6 fusion.42
  526.0 41.6 %psum.23 = f32[2,128]{1,0:T(2,128)} all-reduce(f32[2,128]{1,0:T(2,128)S(1)} %pad_maximum_fusion.3), channel_id=1, replica_groups=mesh['dp'=2,'tm'=8,'height'=2] {'dp','tm','height'}, use_global_device_ids=true, to_apply=%region_13.14 | all-reduce | flops 256 | bytes 2048 | tf_op jit(solution)/shard_map/psum | solution.py:202
  (317 shorter events, 156.7 us)
Async XLA Ops:
  7.2 11.2 %copy-start.8 = (bf16[1,2,8,8,1536]{4,3,2,1,0:T(8,128)(2,1)S(1)}, bf16[1,2,8,8,1536]{4,3,2,1,0:T(8,128)(2,1)}, u32[]{:S(2)}) copy-start(bf16[1,2,8,8,1536]{4,3,2,1,0:T(8,128)(2,1)} %param.14) | copy-start | bytes 1179652
  7.2 508.1 %all-reduce.5.cloned.1.call-start = ((), (), s32[]{:S(2)}) async-start(), calls=%async_computation | async-start | bytes 6291456 | tf_op jit(solution)/shard_map/psum | solution.py:201
  7.9 6.9 %copy-start.18 = (f32[1536]{0:T(1024)}, f32[1536]{0:T(1024)S(1)}, u32[]{:S(2)}) copy-start(f32[1536]{0:T(1024)S(1)} %broadcast_bitcast_fusion.1) | copy-start | bytes 18436
  9.9 17.8 %copy-start.11 = (f32[2,8,8,12]{2,3,1,0:T(8,128)}, f32[2,8,8,12]{2,3,1,0:T(8,128)S(1)}, u32[]{:S(2)}) copy-start(f32[2,8,8,12]{2,3,1,0:T(8,128)S(1)} %get-tuple-element.218) | copy-start | bytes 18436
  9.9 17.8 %copy-start.9 = (bf16[1,2,8,8,1536]{4,3,2,1,0:T(8,128)(2,1)S(1)}, bf16[1,2,8,8,1536]{4,3,2,1,0:T(8,128)(2,1)}, u32[]{:S(2)}) copy-start(bf16[1,2,8,8,1536]{4,3,2,1,0:T(8,128)(2,1)} %param.12) | copy-start | bytes 1179652
  12.3 3.8 collective-permute-start
  14.8 3.6 collective-permute-start.1
  18.4 10.6 %copy-start.13 = (bf16[2,2,4,8,1536]{4,3,2,1,0:T(8,128)(2,1)}, bf16[2,2,4,8,1536]{4,3,2,1,0:T(8,128)(2,1)S(1)}, u32[]{:S(2)}) copy-start(bf16[2,2,4,8,1536]{4,3,2,1,0:T(8,128)(2,1)S(1)} %collective-permute-done.1) | copy-start | bytes 1179652
  19.7 39.2 %collective-permute-start.3 = (bf16[2,2,16,8,1536]{4,3,2,1,0:T(8,128)(2,1)}, bf16[2,2,16,8,1536]{4,3,2,1,0:T(8,128)(2,1)}, u32[]{:S(2)}, u32[]{:S(2)}) collective-permute-start(bf16[2,2,16,8,1536]{4,3,2,1,0:T(8,128)(2,1)} %pad_maximum_fusion.1), channel_id=1, source_target_pairs={{2,0},{4,2},{6,4},{8,6},{10,8},{12,10},{14,12},{3,1},{5,3},{7,5},{... | collective-permute-start | bytes 4718600 | tf_op jit(solution)/shard_map/ppermute | solution.py:20
  21.0 71.8 %collective-permute-start.2 = (bf16[2,2,16,8,1536]{4,3,2,1,0:T(8,128)(2,1)}, bf16[2,2,16,8,1536]{4,3,2,1,0:T(8,128)(2,1)}, u32[]{:S(2)}, u32[]{:S(2)}) collective-permute-start(bf16[2,2,16,8,1536]{4,3,2,1,0:T(8,128)(2,1)} %pad_maximum_fusion.1), channel_id=1, source_target_pairs={{0,2},{2,4},{4,6},{6,8},{8,10},{10,12},{12,14},{1,3},{3,5},{5,7},{... | collective-permute-start | bytes 4718600 | tf_op jit(solution)/shard_map/ppermute | solution.py:19
  27.9 10.8 %copy-start.2 = (f32[128,12,128]{2,1,0:T(8,128)}, f32[128,12,128]{2,1,0:T(8,128)S(1)}, u32[]{:S(2)}) copy-start(f32[128,12,128]{2,1,0:T(8,128)S(1)} %reshape.281) | copy-start | bytes 2359300
  29.0 0.7 copy-start.14
  29.8 8.9 %copy-start.15 = (f32[2,8,8,12]{3,2,1,0:T(8,128)}, f32[2,8,8,12]{3,2,1,0:T(8,128)S(1)}, u32[]{:S(2)}) copy-start(f32[2,8,8,12]{3,2,1,0:T(8,128)S(1)} %copy.91) | copy-start | bytes 18436
  32.2 6.5 %copy-start.22 = (f32[128]{0:T(128)S(1)}, f32[128]{0:T(128)}, u32[]{:S(2)}) copy-start(f32[128]{0:T(128)} %param.17) | copy-start | bytes 1540
  113.2 2.5 copy-start.5
  113.2 2.5 copy-start.20
  113.2 2.5 copy-start.21
  289.4 5.2 copy-start.6
  326.1 3.8 copy-start.1
  330.2 5.6 copy-start
  335.8 156.0 %collective-permute-start.4 = (f32[2,2,16,8,1536]{4,3,2,1,0:T(8,128)}, f32[2,2,16,8,1536]{4,3,2,1,0:T(8,128)S(1)}, u32[]{:S(2)}, u32[]{:S(2)}) collective-permute-start(f32[2,2,16,8,1536]{4,3,2,1,0:T(8,128)} %get-tuple-element.207), channel_id=1, source_target_pairs={{0,2},{2,4},{4,6},{6,8},{8,10},{10,12},{12,14},{1,3},{3,5},{5,7},{... | collective-permute-start | bytes 9437192 | tf_op jit(solution)/shard_map/ppermute | solution.py:19
  340.7 152.9 %collective-permute-start.5 = (f32[2,2,16,8,1536]{4,3,2,1,0:T(8,128)}, f32[2,2,16,8,1536]{4,3,2,1,0:T(8,128)}, u32[]{:S(2)}, u32[]{:S(2)}) collective-permute-start(f32[2,2,16,8,1536]{4,3,2,1,0:T(8,128)} %get-tuple-element.208), channel_id=1, source_target_pairs={{2,0},{4,2},{6,4},{8,6},{10,8},{12,10},{14,12},{3,1},{5,3},{7,5},{... | collective-permute-start | bytes 9437192 | tf_op jit(solution)/shard_map/ppermute | solution.py:20
  491.9 1.7 copy-start.10
  498.4 4.8 copy-start.3
  498.4 4.8 copy-start.7
  498.4 4.8 copy-start.16
  498.4 4.8 copy-start.23
  499.7 21.6 %collective-permute-start.6 = (f32[2,2,4,8,1536]{4,3,2,1,0:T(8,128)}, f32[2,2,4,8,1536]{4,3,2,1,0:T(8,128)}, u32[]{:S(2)}, u32[]{:S(2)}) collective-permute-start(f32[2,2,4,8,1536]{4,3,2,1,0:T(8,128)} %get-tuple-element.211), channel_id=1, source_target_pairs={{0,1},{2,3},{4,5},{6,7},{8,9},{10,11},{12,13},{14,15},{16,17},{18,... | collective-permute-start | bytes 2359304 | tf_op jit(solution)/shard_map/ppermute | solution.py:19
  501.9 19.4 %collective-permute-start.7 = (f32[2,2,4,8,1536]{4,3,2,1,0:T(8,128)}, f32[2,2,4,8,1536]{4,3,2,1,0:T(8,128)}, u32[]{:S(2)}, u32[]{:S(2)}) collective-permute-start(f32[2,2,4,8,1536]{4,3,2,1,0:T(8,128)} %get-tuple-element.212), channel_id=1, source_target_pairs={{1,0},{3,2},{5,4},{7,6},{9,8},{11,10},{13,12},{15,14},{17,16},{19,... | collective-permute-start | bytes 2359304 | tf_op jit(solution)/shard_map/ppermute | solution.py:20
  521.3 1.7 copy-start.4
  521.3 1.7 copy-start.24
  521.3 2.8 copy-start.12
  521.3 2.8 copy-start.17
  521.3 2.8 copy-start.19
  523.3 2.7 copy-start.25
Sparse Core Ops, SparseCore 0:
  350.7 164.4 all-reduce.4
where the time goes:
time: 579 us; the launch traced here: 574 us
  waiting for transfers between devices  196 us (34%)
  local copies, waits for them, and re-layouts  139 us (24%)
  matrix products  95.2 us (16%)
  other arithmetic  66.2 us (11%)
  blocking collectives  41.6 us (7%)
  starting transfers between devices  20.6 us (4%)
  between operations  14.5 us (3%)
    ppermute x4, waiting for transfers between devices, extended(): before = lax.ppermute(last, axis, up)  175 us
    psum x1, blocking collectives, local(): gain_total = lax.psum(gain_terms, ('dp', 'tm', 'height'))  41.6 us
    dynamic_update_slice x36, local copies, waits for them, and re-layouts, attend_all(): lax.map(per_head, (split_heads(query_flat, head_count), split_heads(key_f...  29.8 us
    and x12, other arithmetic, allowed_mask(): video_mask = within & key_valid[None, :]  27.4 us
    unnamed x61, local copies, waits for them, and re-layouts  24.1 us
    dot_general x12, matrix products, head_grads(): jnp.dot(weights_low.T, grad_head, preferred_element_type=jnp.float32)  22.7 us
    ppermute x4, waiting for transfers between devices, extended(): after = lax.ppermute(first, axis, down)  20.7 us
    dot_general x12, matrix products, head_grads(): jnp.dot(weights_low, value_head, preferred_element_type=jnp.float32)  15.8 us
  transfers between devices with their start and end apart: 9, of which 5 were waited for; matrix products, arithmetic and copies ran while one was open for 8% of the time, Pallas kernels for 0%

commit v1 on v0

--- a/solution.py
+++ b/solution.py
@@ -199,7 +199,8 @@
     key_out, key_gain = norm_backward(key_own, key_split, key_inverse, gain_k)
     gain_terms = jnp.stack([query_gain, key_gain])
     text_key_sum, text_value_sum = lax.psum((text_key_part, text_value_part), ("tm", "height"))
-    gain_total = lax.psum(gain_terms, ("dp", "tm", "height"))
+    terms = lax.all_gather(gain_terms, ("dp", "tm", "height"), axis=0, tiled=False)
+    gain_total = terms.sum(axis=0)
     return (
         query_out.astype(jnp.bfloat16)[None],
         key_out.astype(jnp.bfloat16)[None],

time: 579 us -> 578 us (level)
    psum x1 -> x0, blocking collectives: 41.6 us -> none  [local(): gain_total = lax.psum(gain_terms, ('dp', 'tm', 'height'))]
    all_gather x0 -> x1, blocking collectives: none -> 40 us  [local(): lax.all_gather(gain_terms, ('dp', 'tm', 'height'), axis=0, tiled=False)]
where the time goes in v1:
time: 578 us; the launch traced here: 573 us
  waiting for transfers between devices  196 us (34%)
  local copies, waits for them, and re-layouts  139 us (24%)
  matrix products  95.2 us (16%)
  other arithmetic  66.8 us (12%)
  blocking collectives  40 us (7%)
  starting transfers between devices  20.6 us (4%)
  between operations  14.5 us (3%)
    ppermute x4, waiting for transfers between devices, extended(): before = lax.ppermute(last, axis, up)  175 us
    all_gather x1, blocking collectives, local(): lax.all_gather(gain_terms, ('dp', 'tm', 'height'), axis=0, tiled=False)  40 us
    dynamic_update_slice x36, local copies, waits for them, and re-layouts, attend_all(): lax.map(per_head, (split_heads(query_flat, head_count), split_heads(key_f...  29.8 us
    and x12, other arithmetic, allowed_mask(): video_mask = within & key_valid[None, :]  27.4 us
    unnamed x61, local copies, waits for them, and re-layouts  24.1 us
    dot_general x12, matrix products, head_grads(): jnp.dot(weights_low.T, grad_head, preferred_element_type=jnp.float32)  22.7 us
    ppermute x4, waiting for transfers between devices, extended(): after = lax.ppermute(first, axis, down)  20.7 us
    dot_general x12, matrix products, head_grads(): jnp.dot(weights_low, value_head, preferred_element_type=jnp.float32)  15.8 us
  transfers between devices with their start and end apart: 9, of which 5 were waited for; matrix products, arithmetic and copies ran while one was open for 8% of the time, Pallas kernels for 0%

profile of v1, /device:TPU:0, one launch (start us, length us, event | category | flops | bytes accessed | tf_op | source)
XLA Modules:
  0.0 573.4 jit_solution(8663218373155163686)
XLA Ops:
  12.3 2.4 collective-permute-start
  16.1 2.3 collective-permute-done.1
  21.0 6.0 %collective-permute-start.2 = (bf16[2,2,16,8,1536]{4,3,2,1,0:T(8,128)(2,1)}, bf16[2,2,16,8,1536]{4,3,2,1,0:T(8,128)(2,1)}, u32[]{:S(2)}, u32[]{:S(2)}) collective-permute-start(bf16[2,2,16,8,1536]{4,3,2,1,0:T(8,128)(2,1)} %pad_maximum_fusion.1), channel_id=1, source_target_pairs={{0,2},{2,4},{4,6},{6,8},{8,10},{10,12},{12,14},{1,3},{3,5},{5,7},{... | collective-permute-start | bytes 4718600 | tf_op jit(solution)/shard_map/ppermute | solution.py:19
  33.6 1.9 copy.74
  37.0 1.7 copy.76
  40.6 18.4 %collective-permute-done.3 = bf16[2,2,16,8,1536]{4,3,2,1,0:T(8,128)(2,1)} collective-permute-done((bf16[2,2,16,8,1536]{4,3,2,1,0:T(8,128)(2,1)}, bf16[2,2,16,8,1536]{4,3,2,1,0:T(8,128)(2,1)}, u32[]{:S(2)}, u32[]{:S(2)}) %collective-permute-start.3) | collective-permute-done | bytes 1572896 | tf_op jit(solution)/shard_map/ppermute | solution.py:20
  59.0 33.9 %collective-permute-done.2 = bf16[2,2,16,8,1536]{4,3,2,1,0:T(8,128)(2,1)} collective-permute-done((bf16[2,2,16,8,1536]{4,3,2,1,0:T(8,128)(2,1)}, bf16[2,2,16,8,1536]{4,3,2,1,0:T(8,128)(2,1)}, u32[]{:S(2)}, u32[]{:S(2)}) %collective-permute-start.2) | collective-permute-done | bytes 1572896 | tf_op jit(solution)/shard_map/ppermute | solution.py:19
  92.8 3.0 pad_maximum_fusion
  95.8 2.8 fusion.59
  98.6 4.2 concatenate.31
  102.7 1.9 maximum_bitcast_fusion.1
  104.6 2.4 copy.80
  107.1 4.2 concatenate.28
  111.2 1.9 maximum_bitcast_fusion
  113.2 2.5 copy.78
  115.7 173.7 %while.15 = (s32[]{:T(128)}, f32[12,128,128]{2,0,1:T(8,128)S(1)}, f32[12,1024,128]{1,2,0:T(8,128)}, f32[12,1024,128]{1,2,0:T(8,128)}, s32[128,3]{0,1:T(4,128)S(1...) while((s32[]{:T(128)}, f32[12,128,128]{2,0,1:T(8,128)S(1)}, ...), condition=%wide.region_6.7_spmd.clone, body=%wide.region_2.6_spmd.clone.sunk | while | flops 204930944 | bytes 8207186 | solution.py:103
  117.2 2.3 fusion.92
  127.4 1.9 fusion.98
  131.7 2.3 fusion.92
  141.9 1.9 fusion.98
  146.2 2.3 fusion.92
  156.4 1.9 fusion.98
  160.6 2.3 fusion.92
  170.9 1.9 fusion.98
  175.1 2.3 fusion.92
  185.3 1.9 fusion.98
  189.6 2.3 fusion.92
  199.8 1.9 fusion.98
  204.0 2.3 fusion.92
  214.3 1.9 fusion.98
  218.5 2.3 fusion.92
  228.7 1.9 fusion.98
  233.0 2.3 fusion.92
  243.2 1.9 fusion.98
  247.5 2.3 fusion.92
  257.7 1.9 fusion.98
  261.9 2.3 fusion.92
  272.2 1.9 fusion.98
  276.4 2.3 fusion.92
  286.6 1.9 fusion.98
  289.4 5.2 slice.118
  294.5 6.6 %copy.85 = f32[768,12,128]{2,1,0:T(8,128)} copy(f32[768,12,128]{0,2,1:T(8,128)} %slice.118) | data formatting | bytes 9437184 | tf_op jit(solution)/shard_map/slice | solution.py:186
  301.2 6.8 %stack.31 = f32[1,6,16,8,1536]{4,3,2,1,0:T(8,128)} reshape(f32[768,12,128]{2,1,0:T(8,128)} %copy.85) | data formatting | bytes 9437184 | tf_op jit(solution)/shard_map/stack | solution.py:186
  307.9 4.9 slice.119
  312.8 6.6 %copy.87 = f32[768,12,128]{2,1,0:T(8,128)} copy(f32[768,12,128]{0,2,1:T(8,128)} %slice.119) | data formatting | bytes 9437184 | tf_op jit(solution)/shard_map/slice | solution.py:186
  319.4 6.8 %stack.32 = f32[1,6,16,8,1536]{4,3,2,1,0:T(8,128)} reshape(f32[768,12,128]{2,1,0:T(8,128)} %copy.87) | data formatting | bytes 9437184 | tf_op jit(solution)/shard_map/stack | solution.py:186
  326.1 2.8 constant_dynamic-update-slice_fusion.2
  330.2 3.4 fusion.58
  333.6 2.2 copy-done
  335.8 4.8 collective-permute-start.4
  342.0 1.7 copy.88
  345.2 2.7 slice.128
  347.9 2.7 slice.129
  350.6 141.3 %collective-permute-done.4 = f32[2,2,16,8,1536]{4,3,2,1,0:T(8,128)S(1)} collective-permute-done((f32[2,2,16,8,1536]{4,3,2,1,0:T(8,128)}, f32[2,2,16,8,1536]{4,3,2,1,0:T(8,128)S(1)}, u32[]{:S(2)}, u32[]{:S(2)}) %collective-permute-start.4) | collective-permute-done | bytes 3145760 | tf_op jit(solution)/shard_map/ppermute | solution.py:19
  491.9 1.7 copy-done.10
  493.5 4.8 fusion.41
  499.7 2.2 collective-permute-start.6
  508.7 1.6 copy.83
  510.3 2.2 reshape_reshape_reshape.3
  512.6 2.6 fusion.53
  515.2 3.0 copy.89
  518.3 3.0 copy.90
  521.3 1.6 fusion.42
  526.0 40.0 %all-gather.1 = f32[32,2,128]{2,1,0:T(2,128)S(1)} all-gather(f32[1,2,128]{2,1,0:T(2,128)S(1)} %maximum_bitcast_fusion.2), channel_id=2, replica_groups=mesh['dp'=2,'tm'=8,'height'=2] {'dp','tm','height'}, dimensions={0}, use_global_device_ids=true | all-gather | bytes 33792 | tf_op jit(solution)/shard_map/all_gather | solution.py:202
  (318 shorter events, 157.3 us)
Async XLA Ops:
  7.2 11.2 %copy-start.8 = (bf16[1,2,8,8,1536]{4,3,2,1,0:T(8,128)(2,1)S(1)}, bf16[1,2,8,8,1536]{4,3,2,1,0:T(8,128)(2,1)}, u32[]{:S(2)}) copy-start(bf16[1,2,8,8,1536]{4,3,2,1,0:T(8,128)(2,1)} %param.14) | copy-start | bytes 1179652
  7.2 508.1 %all-reduce.5.cloned.1.call-start = ((), (), s32[]{:S(2)}) async-start(), calls=%async_computation | async-start | bytes 6291456 | tf_op jit(solution)/shard_map/psum | solution.py:201
  7.9 6.9 %copy-start.18 = (f32[1536]{0:T(1024)}, f32[1536]{0:T(1024)S(1)}, u32[]{:S(2)}) copy-start(f32[1536]{0:T(1024)S(1)} %broadcast_bitcast_fusion.1) | copy-start | bytes 18436
  9.9 17.8 %copy-start.11 = (f32[2,8,8,12]{2,3,1,0:T(8,128)}, f32[2,8,8,12]{2,3,1,0:T(8,128)S(1)}, u32[]{:S(2)}) copy-start(f32[2,8,8,12]{2,3,1,0:T(8,128)S(1)} %get-tuple-element.218) | copy-start | bytes 18436
  9.9 17.8 %copy-start.9 = (bf16[1,2,8,8,1536]{4,3,2,1,0:T(8,128)(2,1)S(1)}, bf16[1,2,8,8,1536]{4,3,2,1,0:T(8,128)(2,1)}, u32[]{:S(2)}) copy-start(bf16[1,2,8,8,1536]{4,3,2,1,0:T(8,128)(2,1)} %param.12) | copy-start | bytes 1179652
  12.3 3.8 collective-permute-start
  14.8 3.6 collective-permute-start.1
  18.4 10.6 %copy-start.13 = (bf16[2,2,4,8,1536]{4,3,2,1,0:T(8,128)(2,1)}, bf16[2,2,4,8,1536]{4,3,2,1,0:T(8,128)(2,1)S(1)}, u32[]{:S(2)}) copy-start(bf16[2,2,4,8,1536]{4,3,2,1,0:T(8,128)(2,1)S(1)} %collective-permute-done.1) | copy-start | bytes 1179652
  19.7 39.2 %collective-permute-start.3 = (bf16[2,2,16,8,1536]{4,3,2,1,0:T(8,128)(2,1)}, bf16[2,2,16,8,1536]{4,3,2,1,0:T(8,128)(2,1)}, u32[]{:S(2)}, u32[]{:S(2)}) collective-permute-start(bf16[2,2,16,8,1536]{4,3,2,1,0:T(8,128)(2,1)} %pad_maximum_fusion.1), channel_id=1, source_target_pairs={{2,0},{4,2},{6,4},{8,6},{10,8},{12,10},{14,12},{3,1},{5,3},{7,5},{... | collective-permute-start | bytes 4718600 | tf_op jit(solution)/shard_map/ppermute | solution.py:20
  21.0 71.8 %collective-permute-start.2 = (bf16[2,2,16,8,1536]{4,3,2,1,0:T(8,128)(2,1)}, bf16[2,2,16,8,1536]{4,3,2,1,0:T(8,128)(2,1)}, u32[]{:S(2)}, u32[]{:S(2)}) collective-permute-start(bf16[2,2,16,8,1536]{4,3,2,1,0:T(8,128)(2,1)} %pad_maximum_fusion.1), channel_id=1, source_target_pairs={{0,2},{2,4},{4,6},{6,8},{8,10},{10,12},{12,14},{1,3},{3,5},{5,7},{... | collective-permute-start | bytes 4718600 | tf_op jit(solution)/shard_map/ppermute | solution.py:19
  27.9 10.8 %copy-start.2 = (f32[128,12,128]{2,1,0:T(8,128)}, f32[128,12,128]{2,1,0:T(8,128)S(1)}, u32[]{:S(2)}) copy-start(f32[128,12,128]{2,1,0:T(8,128)S(1)} %reshape.281) | copy-start | bytes 2359300
  29.0 0.7 copy-start.14
  29.8 8.9 %copy-start.15 = (f32[2,8,8,12]{3,2,1,0:T(8,128)}, f32[2,8,8,12]{3,2,1,0:T(8,128)S(1)}, u32[]{:S(2)}) copy-start(f32[2,8,8,12]{3,2,1,0:T(8,128)S(1)} %copy.91) | copy-start | bytes 18436
  32.2 6.5 %copy-start.22 = (f32[128]{0:T(128)S(1)}, f32[128]{0:T(128)}, u32[]{:S(2)}) copy-start(f32[128]{0:T(128)} %param.17) | copy-start | bytes 1540
  113.2 2.5 copy-start.5
  113.2 2.5 copy-start.20
  113.2 2.5 copy-start.21
  289.4 5.2 copy-start.6
  326.1 3.8 copy-start.1
  330.2 5.6 copy-start
  335.8 156.0 %collective-permute-start.4 = (f32[2,2,16,8,1536]{4,3,2,1,0:T(8,128)}, f32[2,2,16,8,1536]{4,3,2,1,0:T(8,128)S(1)}, u32[]{:S(2)}, u32[]{:S(2)}) collective-permute-start(f32[2,2,16,8,1536]{4,3,2,1,0:T(8,128)} %get-tuple-element.207), channel_id=1, source_target_pairs={{0,2},{2,4},{4,6},{6,8},{8,10},{10,12},{12,14},{1,3},{3,5},{5,7},{... | collective-permute-start | bytes 9437192 | tf_op jit(solution)/shard_map/ppermute | solution.py:19
  340.7 152.9 %collective-permute-start.5 = (f32[2,2,16,8,1536]{4,3,2,1,0:T(8,128)}, f32[2,2,16,8,1536]{4,3,2,1,0:T(8,128)}, u32[]{:S(2)}, u32[]{:S(2)}) collective-permute-start(f32[2,2,16,8,1536]{4,3,2,1,0:T(8,128)} %get-tuple-element.208), channel_id=1, source_target_pairs={{2,0},{4,2},{6,4},{8,6},{10,8},{12,10},{14,12},{3,1},{5,3},{7,5},{... | collective-permute-start | bytes 9437192 | tf_op jit(solution)/shard_map/ppermute | solution.py:20
  491.9 1.7 copy-start.10
  498.4 4.8 copy-start.3
  498.4 4.8 copy-start.7
  498.4 4.8 copy-start.16
  498.4 4.8 copy-start.23
  499.7 21.6 %collective-permute-start.6 = (f32[2,2,4,8,1536]{4,3,2,1,0:T(8,128)}, f32[2,2,4,8,1536]{4,3,2,1,0:T(8,128)}, u32[]{:S(2)}, u32[]{:S(2)}) collective-permute-start(f32[2,2,4,8,1536]{4,3,2,1,0:T(8,128)} %get-tuple-element.211), channel_id=1, source_target_pairs={{0,1},{2,3},{4,5},{6,7},{8,9},{10,11},{12,13},{14,15},{16,17},{18,... | collective-permute-start | bytes 2359304 | tf_op jit(solution)/shard_map/ppermute | solution.py:19
  501.9 19.4 %collective-permute-start.7 = (f32[2,2,4,8,1536]{4,3,2,1,0:T(8,128)}, f32[2,2,4,8,1536]{4,3,2,1,0:T(8,128)}, u32[]{:S(2)}, u32[]{:S(2)}) collective-permute-start(f32[2,2,4,8,1536]{4,3,2,1,0:T(8,128)} %get-tuple-element.212), channel_id=1, source_target_pairs={{1,0},{3,2},{5,4},{7,6},{9,8},{11,10},{13,12},{15,14},{17,16},{19,... | collective-permute-start | bytes 2359304 | tf_op jit(solution)/shard_map/ppermute | solution.py:20
  521.3 1.7 copy-start.4
  521.3 1.7 copy-start.24
  521.3 2.8 copy-start.12
  521.3 2.8 copy-start.17
  521.3 2.8 copy-start.19
  523.3 2.7 copy-start.25
Sparse Core Ops, SparseCore 0:
  350.7 164.4 all-reduce.4
